TPU v7x, 32 devices: a whole 2x2x4 slice. The times are simulated.
32 devices in a mesh: row: 8 (over z, y), col: 4 (over x, core).
Axes of the slice: x: 2, y: 2, z: 4, core: 2. Of those that a mesh axis runs over, the one named last changes fastest.
Arguments:
- image_states: bfloat16 [64, 3072], P(('row', 'col')), may hold values from -6 to 6
- latent: float32 [64, 64], P(('row', 'col')), may hold values from -6 to 6
- text_keys: bfloat16 [1024, 3072], P('row', 'col')
- text_values: bfloat16 [1024, 3072], P('row', 'col'), may hold values from -6 to 6
- mod_table: float32 [4, 8, 3072], replicated, may hold values from -3 to 3
- timestep: int32 [4], replicated, may hold values from 0 to 3
- grid_size: int32 [4, 2], replicated, may hold values from 1 to 8, as said below
- rope_offset: int32 [4, 2], replicated, may hold values from 0 to 63
- w_qkv: bfloat16 [3072, 9216], P(None, 'row'), may hold values from -0.109375 to 0.109375
- q_gain: float32 [128], replicated, may hold values from 0.1 to 1.9
- k_gain: float32 [128], replicated, may hold values from 0.5 to 4
- w_out: bfloat16 [3072, 3072], P('col', 'row'), may hold values from -0.109375 to 0.109375
- w_fc1: bfloat16 [3072, 12288], P(None, 'row'), may hold values from -0.109375 to 0.109375
- w_fc2: bfloat16 [12288, 3072], P('row'), may hold values from -0.0546875 to 0.0546875
- w_final: bfloat16 [3072, 64], replicated, may hold values from -0.109375 to 0.109375
Outputs:
- velocity: float32 [64, 64], P(('row', 'col'))
- next_latent: float32 [64, 64], P(('row', 'col'))
Inputs may be any that keep to these rules, and one draw needn't show every extreme that they name: `grid_size`: column 0 is a request's grid height, at most 2; column 1 its grid width, at most 8; in every draw some request has height 2 and some request width 8.
All inputs are finite; a program needn't handle non-finite values.
Results may differ from a plain program's by a relative error of at most 0.008.
Values may be sent and summed in bfloat16 or wider, within the bound.
No kernel may reach another device: no remote copies, remote signals or barrier semaphores. Data moves between devices by JAX's collectives and lax.ppermute only.
A program may use at most 128 MiB of HBM per device.

v0:
```python
import jax
import jax.numpy as jnp
from jax import lax
from jax.sharding import PartitionSpec as P

REQ = 4
TXT = 256
STEPS = 4
eps_norm = 1e-06
blend = 0.25
mask_floor = -1e30


def with_halo(cells, sides, width):
    for axis, dim in sides:
        count = lax.axis_size(axis)
        ends = count - 1
        head = lax.slice_in_dim(cells, 0, width, axis=dim)
        tail = lax.slice_in_dim(cells, cells.shape[dim] - width, cells.shape[dim], axis=dim)
        cells = jnp.concatenate(
            [
                lax.ppermute(tail, axis, [(i, (i + 1) % count) for i in range(ends)]),
                cells,
                lax.ppermute(head, axis, [((i + 1) % count, i) for i in range(ends)]),
            ],
            axis=dim,
        )
    return cells


def layer_norm(values):
    mean_value = jnp.mean(values, -1, keepdims=True)
    centred = values - mean_value
    return centred * lax.rsqrt(jnp.mean(centred * centred, -1, keepdims=True) + eps_norm)


def modulate(values, shift_vec, scale_vec):
    return (layer_norm(values) * (1.0 + scale_vec) + shift_vec).astype(jnp.bfloat16)


def rope_tables(pos_h, pos_w, head_size):
    time_half = head_size // 16
    axis_dim = (head_size - head_size // 8) // 2
    freq_index = jnp.arange(axis_dim // 2, dtype=jnp.float32)
    frequency = 10000.0 ** (-2.0 * freq_index / axis_dim)
    angles = jnp.concatenate(
        [
            jnp.zeros((pos_h.shape[0], time_half), jnp.float32),
            pos_h[:, None] * frequency[None, :],
            pos_w[:, None] * frequency[None, :],
        ],
        1,
    )
    return (jnp.cos(angles), jnp.sin(angles))


def norm_rope(values, gain_vec, cosine_table, sine_table, head_count, head_size):
    row_total = values.shape[0]
    per_head = values.astype(jnp.float32).reshape(row_total, head_count, head_size)
    per_head = (
        per_head * lax.rsqrt(jnp.mean(per_head * per_head, -1, keepdims=True) + eps_norm) * gain_vec
    )
    paired = per_head.reshape(row_total, head_count, head_size // 2, 2)
    even_part = paired[..., 0]
    odd_part = paired[..., 1]
    cos_wide = cosine_table[:, None, :]
    sin_wide = sine_table[:, None, :]
    turned = jnp.stack(
        [even_part * cos_wide - odd_part * sin_wide, even_part * sin_wide + odd_part * cos_wide], -1
    )
    return turned.reshape(row_total, head_count * head_size).astype(jnp.bfloat16)


def on_device(
    image_states,
    latent,
    text_keys,
    text_values,
    mod_table,
    timestep,
    grid_size,
    rope_offset,
    w_qkv,
    q_gain,
    k_gain,
    w_out,
    w_fc1,
    w_fc2,
    w_final,
):
    col_total = lax.axis_size("col")
    row_pos = lax.axis_index("row")
    col_pos = lax.axis_index("col")
    tile_w = image_states.shape[0]
    width = image_states.shape[1]
    head_size = q_gain.shape[0]
    head_count = width // head_size
    local_heads = head_count // col_total
    request = row_pos % REQ
    grid_row = row_pos // REQ
    grid_col = col_pos * tile_w + jnp.arange(tile_w, dtype=jnp.int32)
    req_slots = jnp.arange(REQ, dtype=jnp.int32)
    req_onehot = req_slots == request
    limits = jnp.sum(jnp.where(req_onehot[:, None], grid_size, 0), 0)
    offsets = jnp.sum(jnp.where(req_onehot[:, None], rope_offset, 0), 0)
    step_now = jnp.sum(jnp.where(req_onehot, timestep, 0))
    token_ok = (grid_row < limits[0]) & (grid_col < limits[1])
    modulation = lax.dynamic_index_in_dim(mod_table, step_now, 0, keepdims=False)
    states = image_states.astype(jnp.float32)
    normed = modulate(states, modulation[0], modulation[1])
    joined_cols = jnp.dot(
        lax.all_gather(normed, "row", axis=0, tiled=True), w_qkv, preferred_element_type=jnp.float32
    ).astype(jnp.bfloat16)
    joined = lax.all_to_all(joined_cols, "row", split_axis=0, concat_axis=1, tiled=True)
    pos_h = jnp.zeros((tile_w,), jnp.float32) + (grid_row + offsets[0]).astype(jnp.float32)
    pos_w = (grid_col + offsets[1]).astype(jnp.float32)
    cosine_table, sine_table = rope_tables(pos_h, pos_w, head_size)
    queries = norm_rope(joined[:, :width], q_gain, cosine_table, sine_table, head_count, head_size)
    image_keys = norm_rope(
        joined[:, width : 2 * width], k_gain, cosine_table, sine_table, head_count, head_size
    )
    q_heads, k_heads, v_heads = (
        lax.all_to_all(queries, "col", split_axis=1, concat_axis=0, tiled=True),
        lax.all_to_all(image_keys, "col", split_axis=1, concat_axis=0, tiled=True),
        lax.all_to_all(joined[:, 2 * width :], "col", split_axis=1, concat_axis=0, tiled=True),
    )
    image_rows = k_heads.shape[0]
    text_rows = text_keys.shape[0]
    shard_rows = image_rows + text_rows
    q_block = q_heads.reshape(image_rows, local_heads, head_size)
    key_rows = jnp.concatenate([k_heads, text_keys], 0)
    value_rows = jnp.concatenate([v_heads, text_values], 0)
    run_max = jnp.full((image_rows, local_heads), mask_floor, jnp.float32)
    key_piece = lax.all_gather(key_rows, "row", axis=0, tiled=True)
    value_piece = lax.all_gather(value_rows, "row", axis=0, tiled=True)
    piece_rows = key_piece.shape[0]
    global_row = jnp.arange(piece_rows, dtype=jnp.int32)
    shard_id = global_row // shard_rows
    within = global_row % shard_rows
    is_image = within < image_rows
    source_col = within // tile_w
    source_cell = within % tile_w
    image_req = shard_id % REQ
    text_req = (shard_id * text_rows + within - image_rows) // TXT
    key_req = jnp.where(is_image, image_req, text_req)
    key_onehot = key_req[:, None] == req_slots[None, :]
    key_height = jnp.sum(jnp.where(key_onehot, grid_size[:, 0][None, :], 0), 1)
    key_width = jnp.sum(jnp.where(key_onehot, grid_size[:, 1][None, :], 0), 1)
    image_ok = (shard_id // REQ < key_height) & (source_col * tile_w + source_cell < key_width)
    key_ok = (key_req == request) & (jnp.logical_not(is_image) | image_ok)
    scores = jnp.einsum(
        "qhd,khd->qhk",
        q_block,
        key_piece.reshape(piece_rows, local_heads, head_size),
        preferred_element_type=jnp.float32,
    ) * head_size ** (-0.5)
    new_max = jnp.maximum(run_max, jnp.max(jnp.where(key_ok, scores, mask_floor), -1))
    weights = jnp.where(key_ok, jnp.exp(scores - new_max[..., None]), 0.0)
    new_sum = jnp.sum(weights, -1)
    new_acc = jnp.einsum(
        "qhk,khd->qhd",
        weights.astype(jnp.bfloat16),
        value_piece.reshape(piece_rows, local_heads, head_size),
        preferred_element_type=jnp.float32,
    )
    mixed = (
        (new_acc / new_sum[..., None])
        .astype(jnp.bfloat16)
        .reshape(image_rows, local_heads * head_size)
    )
    partial_out = jnp.dot(
        mixed, lax.all_gather(w_out, "row", axis=1, tiled=True), preferred_element_type=jnp.float32
    )
    attended = lax.psum_scatter(
        partial_out.astype(jnp.bfloat16), "col", scatter_dimension=0, tiled=True
    ).astype(jnp.float32)
    first_res = (states + modulation[2] * attended).astype(jnp.bfloat16)
    normed_two = modulate(first_res.astype(jnp.float32), modulation[3], modulation[4])
    all_rows = lax.all_gather(normed_two, "row", axis=0, tiled=True)
    hidden = jax.nn.gelu(
        jnp.dot(all_rows, w_fc1, preferred_element_type=jnp.float32), approximate=True
    ).astype(jnp.bfloat16)
    every_term = jnp.dot(hidden, w_fc2, preferred_element_type=jnp.float32)
    every_sum = lax.psum(every_term, "row")
    mlp_out = lax.dynamic_slice_in_dim(every_sum, row_pos * tile_w, tile_w, 0)
    second_res = first_res.astype(jnp.float32) + modulation[5] * mlp_out
    normed_three = modulate(second_res, modulation[6], modulation[7])
    raw_velocity = jnp.dot(normed_three, w_final, preferred_element_type=jnp.float32)
    masked = jnp.where(token_ok[:, None], raw_velocity, 0.0)
    padded = with_halo(masked, (("col", 0),), 1)
    left_side = padded[:-2]
    right_side = padded[2:]
    velocity = jnp.where(
        token_ok[:, None], masked + blend * (left_side + right_side - 2.0 * masked), 0.0
    )
    next_latent = latent + -1.0 / STEPS * velocity
    return (velocity, next_latent)


def solution(mesh):
    placed = (
        P(("row", "col"), None),
        P(("row", "col"), None),
        P("row", "col"),
        P("row", "col"),
        P(),
        P(),
        P(),
        P(),
        P(None, "row"),
        P(),
        P(),
        P("col", "row"),
        P(None, "row"),
        P("row", None),
        P(),
    )
    return jax.shard_map(
        on_device,
        mesh=mesh,
        in_specs=placed,
        out_specs=(P(("row", "col"), None), P(("row", "col"), None)),
        check_vma=False,
    )
```

profile of v0, /device:TPU:1, one launch (start us, length us, event | category | flops | bytes accessed | tf_op | source)
XLA Modules:
  0.0 413.6 jit_solution(1863781639350607465)
XLA Ops:
  7.2 1.3 select_reduce_fusion.5
  9.8 0.8 convert_reduce_fusion.1
  10.7 0.9 fusion.36
  12.3 2.2 dynamic-slice_add_fusion
  14.5 0.8 fusion.50
  15.3 25.6 %all-gather = bf16[8,2,3072]{2,1,0:T(2,128)(2,1)S(1)} all-gather(bf16[1,2,3072]{2,1,0:T(2,128)(2,1)S(1)} %fusion.50), channel_id=1, replica_groups=mesh['row'=8,'col'=4] {'row'}, dimensions={0}, use_global_device_ids=true | all-gather | bytes 110592 | tf_op jit(solution)/shard_map/all_gather | solution.py:112
  41.0 4.0 convolution_convert_fusion.1
  45.7 5.0 %all-to-all-start = ((bf16[8,2,1152]{2,1,0:T(2,128)(2,1)}), bf16[8,2,1152]{2,1,0:T(2,128)(2,1)S(1)}, u32[]{:S(2)}, u32[]{:S(2)}) async-start(bf16[8,2,1152]{2,1,0:T(2,128)(2,1)} %all_to_all.50), calls=%async_computation | async-start | bytes 73728 | tf_op jit(solution)/shard_map/all_to_all | solution.py:114
  53.2 0.7 mul.324
  53.9 0.7 mul.306
  54.7 1.6 all-to-all-done
  56.9 1.5 reshape.266
  59.2 2.3 reshape.264
  62.2 1.0 multiply_multiply_fusion
  63.3 5.2 %slice_multiply_fusion.5 = (f32[2,24,64,1]{3,2,1,0:T(8,128)}, f32[2,24,64,1]{3,2,1,0:T(8,128)}, f32[2,24,64,1]{3,2,1,0:T(8,128)}, f32[2,24,64,1]{3,2,1,0:T(8,128...) fusion(f32[2,24,64,2]{3,2,1,0:T(8,128)S(1)} %multiply_multiply_, ...), kind=kLoop, calls=%fused_computation.11 | loop fusion | flops 24576 | bytes 148480 | tf_op jit(solution)/shard_map/mul | solution.py:69
  68.5 2.5 copy.52
  71.1 2.5 copy.53
  73.6 2.5 copy.54
  76.1 2.5 copy.55
  78.6 0.8 subtract_convert_fusion.1
  79.4 0.8 add_convert_fusion.2
  80.8 2.0 copy.56
  82.8 2.1 convert_element_type.69
  84.9 14.5 %all_to_all.67 = bf16[2,4,768]{2,0,1:T(2,128)(2,1)} all-to-all(bf16[2,4,768]{2,0,1:T(2,128)(2,1)S(1)} %copy.57), channel_id=1, replica_groups=mesh['row'=8,'col'=4] {'col'}, dimensions={1} | all-to-all | bytes 24576 | tf_op jit(solution)/shard_map/all_to_all | solution.py:124
  100.1 1.6 pad_maximum_fusion.1
  101.8 7.8 %all_to_all.68 = bf16[2,4,768]{2,0,1:T(2,128)(2,1)} all-to-all(bf16[2,4,768]{2,0,1:T(2,128)(2,1)} %bitcast.72), channel_id=1, replica_groups=mesh['row'=8,'col'=4] {'col'}, dimensions={1} | all-to-all | bytes 24576 | tf_op jit(solution)/shard_map/all_to_all | solution.py:125
  110.3 1.6 pad_maximum_fusion
  112.8 2.5 copy.59
  115.4 2.5 copy.60
  117.9 1.1 copy.61
  120.2 1.1 convert_element_type.71
  121.9 3.9 all-to-all-start.3
  127.2 2.2 all-to-all-done.3
  129.4 14.7 %all-gather.8.cloned.1.call-done = bf16[1088,768]{1,0:T(8,128)(2,1)} async-done(((bf16[136,768]{1,0:T(8,128)(2,1)}), bf16[1088,768]{1,0:T(8,128)(2,1)}) %all-gather.8.cloned.1.call-update) | async-done | bytes 1671184 | tf_op jit(solution)/shard_map/all_gather | solution.py:134
  144.1 3.8 copy.58
  147.9 42.3 %all-gather.6.cloned.1.call-done = bf16[1088,768]{1,0:T(8,128)(2,1)} async-done(((bf16[136,768]{1,0:T(8,128)(2,1)}), bf16[1088,768]{1,0:T(8,128)(2,1)}) %all-gather.6.cloned.1.call-update) | async-done | bytes 1671184 | tf_op jit(solution)/shard_map/all_gather | solution.py:135
  190.2 2.7 copy.51
  192.9 1.9 select_reduce_fusion
  195.0 77.3 %all-gather.10.cloned.1.call-done = bf16[768,3072]{1,0:T(8,128)(2,1)} async-done(((bf16[768,384]{1,0:T(8,128)(2,1)}), bf16[768,3072]{1,0:T(8,128)(2,1)}) %all-gather.10.cloned.1.call-update) | async-done | bytes 4718608 | tf_op jit(solution)/shard_map/all_gather | solution.py:172
  272.3 3.7 convolution_convert_fusion
  276.0 11.2 %all-reduce = bf16[8,3072]{1,0:T(8,128)(2,1)S(1)} all-reduce(bf16[8,3072]{1,0:T(8,128)(2,1)S(1)} %convolution_convert_fusion), channel_id=2, replica_groups=mesh['row'=8,'col'=4] {'col'}, use_global_device_ids=true, to_apply=%region_11.12.clone | all-reduce | flops 24576 | bytes 98304
  287.7 24.4 %all-gather.1 = bf16[8,2,3072]{2,1,0:T(2,128)(2,1)S(1)} all-gather(bf16[1,2,3072]{2,1,0:T(2,128)(2,1)S(1)} %fusion.51), channel_id=1, replica_groups=mesh['row'=8,'col'=4] {'row'}, dimensions={0}, use_global_device_ids=true | all-gather | bytes 110592 | tf_op jit(solution)/shard_map/all_gather | solution.py:179
  312.2 9.6 %fusion.22 = f32[16,3072]{1,0:T(8,128)} fusion(bf16[1536,3072]{1,0:T(8,128)(2,1)} %param.28, bf16[16,3072]{1,0:T(8,128)(2,1)S(1)} %reshape.272, bf16[3072,1536]{1,0:T(8,128)(2,1)} %param.27), kind=kOutput, calls=%fused_computation.37 | convolution fusion | flops 302211072 | bytes 19169280 | tf_op jit(solution)/shard_map/dot_general | solution.py:183
  323.0 71.4 %all-reduce.3.cloned.1.call-done = f32[16,3072]{1,0:T(8,128)} async-done(((f32[16,3072]{1,0:T(8,128)}), f32[16,3072]{1,0:T(8,128)}) %all-reduce.3.cloned.1.call-update) | async-done | bytes 196624 | tf_op jit(solution)/shard_map/psum | solution.py:184
  394.4 1.0 fusion.82
  396.0 5.6 %collective-permute-start = (f32[1,64]{1,0:T(1,128)S(1)}, f32[1,64]{1,0:T(1,128)S(1)}, u32[]{:S(2)}, u32[]{:S(2)}) collective-permute-start(f32[1,64]{1,0:T(1,128)S(1)} %get-tuple-element.45), channel_id=1, source_target_pairs={{0,1},{1,2},{2,3},{4,5},{5,6},{6,7},{8,9},{9,10},{10,11},{12,13},{... | collective-permute-start | bytes 776 | tf_op jit(solution)/shard_map/ppermute | solution.py:22
  401.5 1.9 collective-permute-start.1
  403.5 2.9 collective-permute-done.1
  (97 shorter events, 12.7 us)
Async XLA Ops:
  7.2 388.5 %copy-start = (bf16[3072,64]{0,1:T(8,128)(2,1)S(1)}, bf16[3072,64]{0,1:T(8,128)(2,1)}, u32[]{:S(2)}) copy-start(bf16[3072,64]{0,1:T(8,128)(2,1)} %param.29) | copy-start | bytes 1179652
  41.0 9.8 %copy-start.12 = (s32[4,2]{0,1:T(2,128)S(1)}, s32[4,2]{0,1:T(2,128)}, u32[]{:S(2)}) copy-start(s32[4,2]{0,1:T(2,128)} %param.21) | copy-start | bytes 100
  41.0 9.8 %copy-start.13 = (s32[4,2]{0,1:T(2,128)S(1)}, s32[4,2]{0,1:T(2,128)}, u32[]{:S(2)}) copy-start(s32[4,2]{0,1:T(2,128)} %param.22) | copy-start | bytes 100
  41.0 12.1 %copy-start.15 = (f32[128]{0:T(128)S(1)}, f32[128]{0:T(128)}, u32[]{:S(2)}) copy-start(f32[128]{0:T(128)} %param.24) | copy-start | bytes 1540
  41.0 12.9 %copy-start.16 = (f32[128]{0:T(128)S(1)}, f32[128]{0:T(128)}, u32[]{:S(2)}) copy-start(f32[128]{0:T(128)} %param.25) | copy-start | bytes 1540
  45.7 10.6 %all-to-all-start = ((bf16[8,2,1152]{2,1,0:T(2,128)(2,1)}), bf16[8,2,1152]{2,1,0:T(2,128)(2,1)S(1)}, u32[]{:S(2)}, u32[]{:S(2)}) async-start(bf16[8,2,1152]{2,1,0:T(2,128)(2,1)} %all_to_all.50), calls=%async_computation | async-start | bytes 73728 | tf_op jit(solution)/shard_map/all_to_all | solution.py:114
  50.7 93.4 %all-gather.8.cloned.1.call-start = ((), (), s32[]{:S(2)}) async-start(), calls=%async_computation.5 | async-start | bytes 1880064 | tf_op jit(solution)/shard_map/all_gather | solution.py:134
  62.2 1.0 copy-start.2
  101.8 88.4 %all-gather.6.cloned.1.call-start = ((), (), s32[]{:S(2)}) async-start(), calls=%async_computation.4 | async-start | bytes 1880064 | tf_op jit(solution)/shard_map/all_gather | solution.py:135
  111.9 160.4 %all-gather.10.cloned.1.call-start = ((), (), s32[]{:S(2)}) async-start(), calls=%async_computation.6 | async-start | bytes 5308416 | tf_op jit(solution)/shard_map/all_gather | solution.py:172
  119.0 0.7 copy-start.3
  119.0 0.8 copy-start.4
  119.0 0.8 copy-start.5
  119.0 6.9 %copy-start.17 = (u32[32]{0:T(128)S(1)}, u32[32]{0:T(128)}, u32[]{:S(2)}) copy-start(u32[32]{0:T(128)} %constant.158) | copy-start | bytes 388
  121.9 7.5 %all-to-all-start.3 = ((bf16[2,4,768]{2,0,1:T(2,128)(2,1)}), bf16[2,4,768]{2,0,1:T(2,128)(2,1)S(1)}, u32[]{:S(2)}, u32[]{:S(2)}) async-start(bf16[2,4,768]{2,0,1:T(2,128)(2,1)} %copy.64), calls=%async_computation.3 | async-start | bytes 24576 | tf_op jit(solution)/shard_map/all_to_all | solution.py:123
  125.9 268.5 %all-reduce.3.cloned.1.call-start = ((), (), s32[]{:S(2)}) async-start(), calls=%async_computation.7 | async-start | bytes 393216 | tf_op jit(solution)/shard_map/psum | solution.py:184
  272.3 14.9 %copy-start.1 = (bf16[2,3072]{1,0:T(2,128)(2,1)S(1)}, bf16[2,3072]{1,0:T(2,128)(2,1)}, u32[]{:S(2)}) copy-start(bf16[2,3072]{1,0:T(2,128)(2,1)} %param.15) | copy-start | bytes 36868
  272.3 14.9 %copy-start.9 = (f32[1,1,3072]{2,1,0:T(1,128)S(1)}, f32[1,1,3072]{2,1,0:T(1,128)}, u32[]{:S(2)}) copy-start(f32[1,1,3072]{2,1,0:T(1,128)} %get-tuple-element.30) | copy-start | bytes 36868
  272.3 15.3 %copy-start.7 = (f32[1,1,3072]{2,1,0:T(1,128)S(1)}, f32[1,1,3072]{2,1,0:T(1,128)}, u32[]{:S(2)}) copy-start(f32[1,1,3072]{2,1,0:T(1,128)} %get-tuple-element.25) | copy-start | bytes 36868
  272.3 15.3 %copy-start.8 = (f32[1,1,3072]{2,1,0:T(1,128)S(1)}, f32[1,1,3072]{2,1,0:T(1,128)}, u32[]{:S(2)}) copy-start(f32[1,1,3072]{2,1,0:T(1,128)} %get-tuple-element.26) | copy-start | bytes 36868
  312.1 82.3 %copy-start.6 = (f32[1,1,3072]{2,1,0:T(1,128)S(1)}, f32[1,1,3072]{2,1,0:T(1,128)}, u32[]{:S(2)}) copy-start(f32[1,1,3072]{2,1,0:T(1,128)} %get-tuple-element.27) | copy-start | bytes 36868
  312.1 83.6 %copy-start.10 = (f32[1,1,3072]{2,1,0:T(1,128)S(1)}, f32[1,1,3072]{2,1,0:T(1,128)}, u32[]{:S(2)}) copy-start(f32[1,1,3072]{2,1,0:T(1,128)} %get-tuple-element.24) | copy-start | bytes 36868
  312.1 83.6 %copy-start.11 = (f32[1,1,3072]{2,1,0:T(1,128)S(1)}, f32[1,1,3072]{2,1,0:T(1,128)}, u32[]{:S(2)}) copy-start(f32[1,1,3072]{2,1,0:T(1,128)} %get-tuple-element.31) | copy-start | bytes 36868
  312.1 94.3 %copy-start.14 = (f32[2,64]{1,0:T(2,128)S(1)}, f32[2,64]{1,0:T(2,128)}, u32[]{:S(2)}) copy-start(f32[2,64]{1,0:T(2,128)} %param.16) | copy-start | bytes 1540
  396.0 7.5 %collective-permute-start = (f32[1,64]{1,0:T(1,128)S(1)}, f32[1,64]{1,0:T(1,128)S(1)}, u32[]{:S(2)}, u32[]{:S(2)}) collective-permute-start(f32[1,64]{1,0:T(1,128)S(1)} %get-tuple-element.45), channel_id=1, source_target_pairs={{0,1},{1,2},{2,3},{4,5},{5,6},{6,7},{8,9},{9,10},{10,11},{12,13},{... | collective-permute-start | bytes 776 | tf_op jit(solution)/shard_map/ppermute | solution.py:22
  401.5 4.9 %collective-permute-start.1 = (f32[1,64]{1,0:T(1,128)S(1)}, f32[1,64]{1,0:T(1,128)S(1)}, u32[]{:S(2)}, u32[]{:S(2)}) collective-permute-start(f32[1,64]{1,0:T(1,128)S(1)} %get-tuple-element.46), channel_id=1, source_target_pairs={{1,0},{2,1},{3,2},{5,4},{6,5},{7,6},{9,8},{10,9},{11,10},{13,12},{... | collective-permute-start | bytes 776 | tf_op jit(solution)/shard_map/ppermute | solution.py:24
Sparse Core Ops, SparseCore 0:
  101.9 42.1 all-gather.7
  146.3 43.8 all-gather.5
  192.3 79.9 all-gather.9
  321.9 72.4 all-reduce.2
where the time goes:
time: 415 us; the launch traced here: 414 us
  waiting for transfers between devices  213 us (51%)
  blocking collectives  83.5 us (20%)
  local copies, waits for them, and re-layouts  38.6 us (9%)
  other arithmetic  24.4 us (6%)
  matrix products  19.5 us (5%)
  between operations  18 us (4%)
  starting transfers between devices  16.5 us (4%)
    all_gather x1, waiting for transfers between devices, on_device(): lax.all_gather(w_out, 'row', axis=1, tiled=True)  77.3 us
    psum x1, waiting for transfers between devices, on_device(): every_sum = lax.psum(every_term, 'row')  71.4 us
    all_gather x1, waiting for transfers between devices, on_device(): value_piece = lax.all_gather(value_rows, 'row', axis=0, tiled=True)  42.3 us
    all_gather x1, blocking collectives, on_device(): lax.all_gather(normed, 'row', axis=0, tiled=True)  25.6 us
    all_gather x1, blocking collectives, on_device(): all_rows = lax.all_gather(normed_two, 'row', axis=0, tiled=True)  24.4 us
    all_gather x1, waiting for transfers between devices, on_device(): key_piece = lax.all_gather(key_rows, 'row', axis=0, tiled=True)  14.7 us
    all_to_all x1, blocking collectives, on_device(): lax.all_to_all(image_keys, 'col', split_axis=1, concat_axis=0, tiled=True)  14.5 us
    unnamed x1, blocking collectives  11.2 us
  transfers between devices with their start and end apart: 8, of which 7 were waited for; matrix products, arithmetic and copies ran while one was open for 6% of the time, Pallas kernels for 0%

commit v1 on v0

--- a/solution.py
+++ b/solution.py
@@ -131,8 +131,11 @@
     key_rows = jnp.concatenate([k_heads, text_keys], 0)
     value_rows = jnp.concatenate([v_heads, text_values], 0)
     run_max = jnp.full((image_rows, local_heads), mask_floor, jnp.float32)
-    key_piece = lax.all_gather(key_rows, "row", axis=0, tiled=True)
-    value_piece = lax.all_gather(value_rows, "row", axis=0, tiled=True)
+    key_piece, value_piece = jnp.split(
+        lax.all_gather(jnp.concatenate([key_rows, value_rows], 1), "row", axis=0, tiled=True),
+        [key_rows.shape[1]],
+        1,
+    )
     piece_rows = key_piece.shape[0]
     global_row = jnp.arange(piece_rows, dtype=jnp.int32)
     shard_id = global_row // shard_rows

time: 415 us -> 398 us (0.959)
  waiting for transfers between devices: 213 us -> 194 us
  blocking collectives: 83.5 us -> 75.8 us
  local copies, waits for them, and re-layouts: 38.6 us -> 43.5 us
  starting transfers between devices: 16.5 us -> 20.9 us
    all_gather x2 -> x1, waiting for transfers between devices: 56.9 us -> 42.1 us  [on_device(): lax.all_gather(jnp.concatenate([key_rows, value_rows], 1), 'row', axis=0,...]
    split x0 -> x3, local copies, waits for them, and re-layouts: none -> 8.37 us  [on_device(): jnp.split(lax.all_gather(jnp.concatenate([key_rows, value_rows], 1), 'row...]
    all_to_all x1 -> x0, blocking collectives: 7.75 us -> none  [on_device(): lax.all_to_all(joined[:, 2 * width:], 'col', split_axis=1, concat_axis=0,...]
    all_gather x2 -> x0, local copies, waits for them, and re-layouts: 6.55 us -> none  [the longest x1 3.84 us: on_device(): key_piece = lax.all_gather(key_rows, 'row', axis=0, tiled=True)]
    all_gather x1, waiting for transfers between devices: 77.3 us -> 71.7 us  [on_device(): lax.all_gather(w_out, 'row', axis=1, tiled=True)]
    all_to_all x0 -> x1, starting transfers between devices: none -> 4.38 us  [on_device(): lax.all_to_all(joined[:, 2 * width:], 'col', split_axis=1, concat_axis=0,...]
where the time goes in v1:
time: 398 us; the launch traced here: 397 us
  waiting for transfers between devices  194 us (49%)
  blocking collectives  75.8 us (19%)
  local copies, waits for them, and re-layouts  43.5 us (11%)
  other arithmetic  24.8 us (6%)
  starting transfers between devices  20.9 us (5%)
  matrix products  19.6 us (5%)
  between operations  18 us (5%)
    all_gather x1, waiting for transfers between devices, on_device(): lax.all_gather(w_out, 'row', axis=1, tiled=True)  71.7 us
    psum x1, waiting for transfers between devices, on_device(): every_sum = lax.psum(every_term, 'row')  71.4 us
    all_gather x1, waiting for transfers between devices, on_device(): lax.all_gather(jnp.concatenate([key_rows, value_rows], 1), 'row', axis=0,...  42.1 us
    all_gather x1, blocking collectives, on_device(): lax.all_gather(normed, 'row', axis=0, tiled=True)  25.6 us
    all_gather x1, blocking collectives, on_device(): all_rows = lax.all_gather(normed_two, 'row', axis=0, tiled=True)  24.4 us
    all_to_all x1, blocking collectives, on_device(): lax.all_to_all(image_keys, 'col', split_axis=1, concat_axis=0, tiled=True)  14.5 us
    unnamed x1, blocking collectives  11.2 us
    dot_general x1, matrix products, on_device(): every_term = jnp.dot(hidden, w_fc2, preferred_element_type=jnp.float32)  9.62 us
  transfers between devices with their start and end apart: 8, of which 7 were waited for; matrix products, arithmetic and copies ran while one was open for 6% of the time, Pallas kernels for 0%

profile of v1, /device:TPU:1, one launch (start us, length us, event | category | flops | bytes accessed | tf_op | source)
XLA Modules:
  0.0 396.6 jit_solution(10871724446155968353)
XLA Ops:
  7.2 1.3 select_reduce_fusion.5
  9.8 0.8 convert_reduce_fusion.1
  10.7 0.9 fusion.36
  12.3 2.2 dynamic-slice_add_fusion
  14.5 0.8 fusion.50
  15.3 25.6 %all-gather = bf16[8,2,3072]{2,1,0:T(2,128)(2,1)S(1)} all-gather(bf16[1,2,3072]{2,1,0:T(2,128)(2,1)S(1)} %fusion.50), channel_id=1, replica_groups=mesh['row'=8,'col'=4] {'row'}, dimensions={0}, use_global_device_ids=true | all-gather | bytes 110592 | tf_op jit(solution)/shard_map/all_gather | solution.py:112
  41.0 4.0 %convolution_convert_fusion.1 = bf16[16,1152]{1,0:T(8,128)(2,1)S(1)} fusion(bf16[16,3072]{1,0:T(8,128)(2,1)S(1)} %reshape.270, bf16[3072,1152]{1,0:T(8,128)(2,1)} %param.23), kind=kOutput, calls=%fused_computation.3 | convolution fusion | flops 113264640 | bytes 7213056 | tf_op jit(solution)/shard_map/dot_general | solution.py:111
  45.7 5.0 %all-to-all-start = ((bf16[8,2,1152]{2,1,0:T(2,128)(2,1)}), bf16[8,2,1152]{2,1,0:T(2,128)(2,1)S(1)}, u32[]{:S(2)}, u32[]{:S(2)}) async-start(bf16[8,2,1152]{2,1,0:T(2,128)(2,1)} %all_to_all.50), calls=%async_computation | async-start | bytes 73728 | tf_op jit(solution)/shard_map/all_to_all | solution.py:114
  55.2 1.1 all-to-all-done
  57.0 1.5 reshape.266
  59.8 2.3 reshape.263
  62.8 1.0 multiply_multiply_fusion
  64.4 5.3 %slice_multiply_fusion.5 = (f32[2,24,64,1]{3,2,1,0:T(8,128)}, f32[2,24,64,1]{3,2,1,0:T(8,128)}, f32[2,24,64,1]{3,2,1,0:T(8,128)}, f32[2,24,64,1]{3,2,1,0:T(8,128...) fusion(f32[2,24,64,2]{3,2,1,0:T(8,128)S(1)} %multiply_multiply_, ...), kind=kLoop, calls=%fused_computation.11 | loop fusion | flops 24576 | bytes 148480 | tf_op jit(solution)/shard_map/mul | solution.py:69
  69.7 2.5 copy.50
  72.2 2.5 copy.51
  74.8 2.5 copy.52
  77.3 2.5 copy.53
  79.8 0.8 subtract_convert_fusion.1
  80.6 0.8 add_convert_fusion.2
  82.0 2.0 copy.54
  84.0 2.7 convert_element_type.69
  87.4 14.5 %all_to_all.67 = bf16[2,4,768]{2,0,1:T(2,128)(2,1)} all-to-all(bf16[2,4,768]{2,0,1:T(2,128)(2,1)S(1)} %copy.55), channel_id=1, replica_groups=mesh['row'=8,'col'=4] {'col'}, dimensions={1} | all-to-all | bytes 24576 | tf_op jit(solution)/shard_map/all_to_all | solution.py:124
  101.9 4.4 %all-to-all-start.2 = ((bf16[2,4,768]{2,0,1:T(2,128)(2,1)}), bf16[2,4,768]{2,0,1:T(2,128)(2,1)}, u32[]{:S(2)}, u32[]{:S(2)}) async-start(bf16[2,4,768]{2,0,1:T(2,128)(2,1)} %bitcast.72), calls=%async_computation.2 | async-start | bytes 24576 | tf_op jit(solution)/shard_map/all_to_all | solution.py:125
  106.3 1.3 all_to_all.56
  107.6 1.9 all-to-all-done.2
  109.5 1.3 all_to_all.60
  110.9 1.8 maximum_maximum_fusion
  114.2 2.5 copy.59
  116.7 2.5 copy.60
  119.3 1.1 copy.61
  121.6 1.1 convert_element_type.71
  123.3 4.0 all-to-all-start.3
  128.6 2.2 all-to-all-done.3
  130.8 42.1 %all-gather.5.cloned.1.call-done = bf16[1088,1536]{1,0:T(8,128)(2,1)} async-done(((bf16[136,1536]{1,0:T(8,128)(2,1)}), bf16[1088,1536]{1,0:T(8,128)(2,1)}) %all-gather.5.cloned.1.call-update) | async-done | bytes 3342352 | tf_op jit(solution)/shard_map/all_gather | solution.py:135
  173.0 3.4 fusion.84
  176.4 2.2 copy.58
  178.6 2.7 copy.57
  181.3 2.0 select_reduce_fusion
  183.6 71.7 %all-gather.7.cloned.1.call-done = bf16[768,3072]{1,0:T(8,128)(2,1)} async-done(((bf16[768,384]{1,0:T(8,128)(2,1)}), bf16[768,3072]{1,0:T(8,128)(2,1)}) %all-gather.7.cloned.1.call-update) | async-done | bytes 4718608 | tf_op jit(solution)/shard_map/all_gather | solution.py:175
  255.3 3.7 convolution_convert_fusion
  259.0 11.2 %all-reduce = bf16[8,3072]{1,0:T(8,128)(2,1)S(1)} all-reduce(bf16[8,3072]{1,0:T(8,128)(2,1)S(1)} %convolution_convert_fusion), channel_id=2, replica_groups=mesh['row'=8,'col'=4] {'col'}, use_global_device_ids=true, to_apply=%region_11.12.clone | all-reduce | flops 24576 | bytes 98304
  270.7 24.4 %all-gather.1 = bf16[8,2,3072]{2,1,0:T(2,128)(2,1)S(1)} all-gather(bf16[1,2,3072]{2,1,0:T(2,128)(2,1)S(1)} %fusion.51), channel_id=1, replica_groups=mesh['row'=8,'col'=4] {'row'}, dimensions={0}, use_global_device_ids=true | all-gather | bytes 110592 | tf_op jit(solution)/shard_map/all_gather | solution.py:182
  295.2 9.6 %fusion.22 = f32[16,3072]{1,0:T(8,128)} fusion(bf16[1536,3072]{1,0:T(8,128)(2,1)} %param.28, bf16[16,3072]{1,0:T(8,128)(2,1)S(1)} %reshape.272, bf16[3072,1536]{1,0:T(8,128)(2,1)} %param.27), kind=kOutput, calls=%fused_computation.36 | convolution fusion | flops 302211072 | bytes 19169280 | tf_op jit(solution)/shard_map/dot_general | solution.py:186
  306.0 71.4 %all-reduce.3.cloned.1.call-done = f32[16,3072]{1,0:T(8,128)} async-done(((f32[16,3072]{1,0:T(8,128)}), f32[16,3072]{1,0:T(8,128)}) %all-reduce.3.cloned.1.call-update) | async-done | bytes 196624 | tf_op jit(solution)/shard_map/psum | solution.py:187
  377.4 1.0 fusion.82
  379.0 5.6 %collective-permute-start = (f32[1,64]{1,0:T(1,128)S(1)}, f32[1,64]{1,0:T(1,128)S(1)}, u32[]{:S(2)}, u32[]{:S(2)}) collective-permute-start(f32[1,64]{1,0:T(1,128)S(1)} %get-tuple-element.47), channel_id=1, source_target_pairs={{0,1},{1,2},{2,3},{4,5},{5,6},{6,7},{8,9},{9,10},{10,11},{12,13},{... | collective-permute-start | bytes 776 | tf_op jit(solution)/shard_map/ppermute | solution.py:22
  384.6 1.9 collective-permute-start.1
  386.5 2.9 collective-permute-done.1
  (101 shorter events, 15.6 us)
Async XLA Ops:
  7.2 371.5 %copy-start = (bf16[3072,64]{0,1:T(8,128)(2,1)S(1)}, bf16[3072,64]{0,1:T(8,128)(2,1)}, u32[]{:S(2)}) copy-start(bf16[3072,64]{0,1:T(8,128)(2,1)} %param.29) | copy-start | bytes 1179652
  41.0 9.8 %copy-start.14 = (s32[4,2]{0,1:T(2,128)S(1)}, s32[4,2]{0,1:T(2,128)}, u32[]{:S(2)}) copy-start(s32[4,2]{0,1:T(2,128)} %param.21) | copy-start | bytes 100
  41.0 9.8 %copy-start.16 = (s32[4,2]{0,1:T(2,128)S(1)}, s32[4,2]{0,1:T(2,128)}, u32[]{:S(2)}) copy-start(s32[4,2]{0,1:T(2,128)} %param.22) | copy-start | bytes 100
  41.0 12.7 %copy-start.18 = (f32[128]{0:T(128)S(1)}, f32[128]{0:T(128)}, u32[]{:S(2)}) copy-start(f32[128]{0:T(128)} %param.24) | copy-start | bytes 1540
  41.0 13.4 %copy-start.19 = (f32[128]{0:T(128)S(1)}, f32[128]{0:T(128)}, u32[]{:S(2)}) copy-start(f32[128]{0:T(128)} %param.25) | copy-start | bytes 1540
  45.7 10.6 %all-to-all-start = ((bf16[8,2,1152]{2,1,0:T(2,128)(2,1)}), bf16[8,2,1152]{2,1,0:T(2,128)(2,1)S(1)}, u32[]{:S(2)}, u32[]{:S(2)}) async-start(bf16[8,2,1152]{2,1,0:T(2,128)(2,1)} %all_to_all.50), calls=%async_computation | async-start | bytes 73728 | tf_op jit(solution)/shard_map/all_to_all | solution.py:114
  62.8 1.0 copy-start.2
  63.7 0.7 copy-start.13
  84.0 29.5 %copy-start.15 = (s32[4,2]{0,1:T(2,128)S(1)}, s32[4,2]{0,1:T(2,128)}, u32[]{:S(2)}) copy-start(s32[4,2]{0,1:T(2,128)} %param.21) | copy-start | bytes 100
  101.9 7.6 %all-to-all-start.2 = ((bf16[2,4,768]{2,0,1:T(2,128)(2,1)}), bf16[2,4,768]{2,0,1:T(2,128)(2,1)}, u32[]{:S(2)}, u32[]{:S(2)}) async-start(bf16[2,4,768]{2,0,1:T(2,128)(2,1)} %bitcast.72), calls=%async_computation.2 | async-start | bytes 24576 | tf_op jit(solution)/shard_map/all_to_all | solution.py:125
  106.3 66.7 %all-gather.5.cloned.1.call-start = ((), (), s32[]{:S(2)}) async-start(), calls=%async_computation.4 | async-start | bytes 3760128 | tf_op jit(solution)/shard_map/all_gather | solution.py:135
  112.7 142.6 %all-gather.7.cloned.1.call-start = ((), (), s32[]{:S(2)}) async-start(), calls=%async_computation.5 | async-start | bytes 5308416 | tf_op jit(solution)/shard_map/all_gather | solution.py:175
  120.4 0.7 copy-start.3
  120.4 0.8 copy-start.4
  120.4 0.8 copy-start.5
  120.4 6.9 %copy-start.9 = (s32[1088]{0:T(1024)S(1)}, s32[1088]{0:T(1024)}, u32[]{:S(2)}) copy-start(s32[1088]{0:T(1024)} %get-tuple-element.2) | copy-start | bytes 13060
  120.4 6.9 %copy-start.10 = (s32[1088]{0:T(1024)S(1)}, s32[1088]{0:T(1024)}, u32[]{:S(2)}) copy-start(s32[1088]{0:T(1024)} %get-tuple-element.3) | copy-start | bytes 13060
  120.4 6.9 %copy-start.20 = (u32[32]{0:T(128)S(1)}, u32[32]{0:T(128)}, u32[]{:S(2)}) copy-start(u32[32]{0:T(128)} %constant.158) | copy-start | bytes 388
  123.3 7.5 %all-to-all-start.3 = ((bf16[2,4,768]{2,0,1:T(2,128)(2,1)}), bf16[2,4,768]{2,0,1:T(2,128)(2,1)S(1)}, u32[]{:S(2)}, u32[]{:S(2)}) async-start(bf16[2,4,768]{2,0,1:T(2,128)(2,1)} %copy.64), calls=%async_computation.3 | async-start | bytes 24576 | tf_op jit(solution)/shard_map/all_to_all | solution.py:123
  127.3 250.1 %all-reduce.3.cloned.1.call-start = ((), (), s32[]{:S(2)}) async-start(), calls=%async_computation.6 | async-start | bytes 393216 | tf_op jit(solution)/shard_map/psum | solution.py:187
  255.3 14.9 %copy-start.1 = (bf16[2,3072]{1,0:T(2,128)(2,1)S(1)}, bf16[2,3072]{1,0:T(2,128)(2,1)}, u32[]{:S(2)}) copy-start(bf16[2,3072]{1,0:T(2,128)(2,1)} %param.15) | copy-start | bytes 36868
  255.3 14.9 %copy-start.8 = (f32[1,1,3072]{2,1,0:T(1,128)S(1)}, f32[1,1,3072]{2,1,0:T(1,128)}, u32[]{:S(2)}) copy-start(f32[1,1,3072]{2,1,0:T(1,128)} %get-tuple-element.32) | copy-start | bytes 36868
  255.3 15.3 %copy-start.6 = (f32[1,1,3072]{2,1,0:T(1,128)S(1)}, f32[1,1,3072]{2,1,0:T(1,128)}, u32[]{:S(2)}) copy-start(f32[1,1,3072]{2,1,0:T(1,128)} %get-tuple-element.27) | copy-start | bytes 36868
  255.3 15.3 %copy-start.7 = (f32[1,1,3072]{2,1,0:T(1,128)S(1)}, f32[1,1,3072]{2,1,0:T(1,128)}, u32[]{:S(2)}) copy-start(f32[1,1,3072]{2,1,0:T(1,128)} %get-tuple-element.28) | copy-start | bytes 36868
  295.1 83.6 %copy-start.11 = (f32[1,1,3072]{2,1,0:T(1,128)S(1)}, f32[1,1,3072]{2,1,0:T(1,128)}, u32[]{:S(2)}) copy-start(f32[1,1,3072]{2,1,0:T(1,128)} %get-tuple-element.26) | copy-start | bytes 36868
  295.2 83.6 %copy-start.12 = (f32[1,1,3072]{2,1,0:T(1,128)S(1)}, f32[1,1,3072]{2,1,0:T(1,128)}, u32[]{:S(2)}) copy-start(f32[1,1,3072]{2,1,0:T(1,128)} %get-tuple-element.33) | copy-start | bytes 36868
  295.2 94.3 %copy-start.17 = (f32[2,64]{1,0:T(2,128)S(1)}, f32[2,64]{1,0:T(2,128)}, u32[]{:S(2)}) copy-start(f32[2,64]{1,0:T(2,128)} %param.16) | copy-start | bytes 1540
  379.0 7.5 %collective-permute-start = (f32[1,64]{1,0:T(1,128)S(1)}, f32[1,64]{1,0:T(1,128)S(1)}, u32[]{:S(2)}, u32[]{:S(2)}) collective-permute-start(f32[1,64]{1,0:T(1,128)S(1)} %get-tuple-element.47), channel_id=1, source_target_pairs={{0,1},{1,2},{2,3},{4,5},{5,6},{6,7},{8,9},{9,10},{10,11},{12,13},{... | collective-permute-start | bytes 776 | tf_op jit(solution)/shard_map/ppermute | solution.py:22
  384.6 4.9 %collective-permute-start.1 = (f32[1,64]{1,0:T(1,128)S(1)}, f32[1,64]{1,0:T(1,128)S(1)}, u32[]{:S(2)}, u32[]{:S(2)}) collective-permute-start(f32[1,64]{1,0:T(1,128)S(1)} %get-tuple-element.48), channel_id=1, source_target_pairs={{1,0},{2,1},{3,2},{5,4},{6,5},{7,6},{9,8},{10,9},{11,10},{13,12},{... | collective-permute-start | bytes 776 | tf_op jit(solution)/shard_map/ppermute | solution.py:24
Sparse Core Ops, SparseCore 0:
  112.8 60.0 all-gather.4
  175.0 80.2 all-gather.6
  304.9 72.4 all-reduce.2
